TPU v7x, 32 devices: a whole 2x2x4 slice. The times are simulated.
32 devices in a mesh: row: 4 (over z), col: 4 (over y, x), agent: 2 (over core).
Axes of the slice: x: 2, y: 2, z: 4, core: 2. Of those that a mesh axis runs over, the one named last changes fastest.
Arguments:
- raster: bfloat16 [2, 512, 512, 128], P(None, 'row', ('col', 'agent')), may hold values from -6 to 6
- first_kernel: bfloat16 [3, 3, 128, 128], replicated, may hold values from -0.1875 to 0.1875
- first_bias: float32 [128], replicated, may hold values from -3 to 3
- second_kernel: bfloat16 [3, 3, 128, 128], replicated, may hold values from -0.1875 to 0.1875
- second_bias: float32 [128], replicated, may hold values from -3 to 3
- queries: bfloat16 [256, 128], P('agent'), may hold values from -64 to 64
- agent_slot: int32 [256], replicated, may hold values from 0 to 255, each once
- regions: int32 [256, 4], replicated, may hold values from 0 to 8, as said below
Outputs:
- log_heatmap: float32 [2, 512, 512, 256], P(None, 'row', ('col', 'agent'))
Inputs may be any that keep to these rules, and one draw needn't show every extreme that they name: regions[a,0] < regions[a,1] <= 8 and regions[a,2] < regions[a,3] <= 8.
All inputs are finite; a program needn't handle non-finite values.
Results may differ from a plain program's by a relative error of at most 0.0024.
Values may be sent and summed in bfloat16 or wider, within the bound.
A program may use at most 192 MiB of HBM per device.

v0:
```python
import jax
import jax.numpy as jnp
from jax import lax
from jax.sharding import PartitionSpec as P

BLOCK = 64


def padded_2(block, sides, width):
    for axis, dim in sides:
        count = lax.axis_size(axis)
        forward = [(i, i + 1) for i in range(count - 1)]
        backward = [(target, source) for source, target in forward]
        low = lax.ppermute(
            lax.slice_in_dim(block, block.shape[dim] - width, None, axis=dim), axis, forward
        )
        high = lax.ppermute(lax.slice_in_dim(block, 0, width, axis=dim), axis, backward)
        block = jnp.concatenate([low, block, high], axis=dim)
    return block


def dilated(padded, kernel, bias, dilation, out_rows, out_cols):
    scenes = padded.shape[0]
    channels = padded.shape[3]
    running = jnp.zeros((scenes * out_rows * out_cols, kernel.shape[3]), jnp.float32)
    for row_tap in range(3):
        for col_tap in range(3):
            tap_piece = padded[
                :,
                row_tap * dilation : row_tap * dilation + out_rows,
                col_tap * dilation : col_tap * dilation + out_cols,
                :,
            ]
            running = running + jnp.dot(
                tap_piece.reshape(-1, channels),
                kernel[row_tap, col_tap],
                preferred_element_type=jnp.float32,
            )
    result = jnp.maximum(running + bias, 0.0).astype(jnp.bfloat16)
    return result.reshape(scenes, out_rows, out_cols, -1)


def shards(
    raster, first_kernel, first_bias, second_kernel, second_bias, queries, agent_slot, regions
):
    scenes, tile_rows, tile_cols, channels = raster.shape
    row_start = lax.axis_index("row") * tile_rows
    col_start = lax.axis_index(("col", "agent")) * tile_cols
    near_field = padded_2(raster, (("row", 1), (("col", "agent"), 2)), 4)
    layer_one = dilated(near_field, first_kernel, first_bias, 4, tile_rows, tile_cols)
    far_field = padded_2(layer_one, (("row", 1), (("col", "agent"), 2)), 8)
    layer_two = dilated(far_field, second_kernel, second_bias, 8, tile_rows, tile_cols)
    everyone = lax.all_gather(queries, "agent", axis=0, tiled=True)
    ordered = jnp.take(everyone, agent_slot, axis=0)
    agents = ordered.shape[0]
    flat = layer_two.reshape(scenes, tile_rows * tile_cols, channels)
    logits = jnp.einsum("snc,ac->sna", flat, ordered, preferred_element_type=jnp.float32)
    block_rows = (row_start + jnp.arange(tile_rows, dtype=jnp.int32)) // BLOCK
    block_cols = (col_start + jnp.arange(tile_cols, dtype=jnp.int32)) // BLOCK
    row_ok = (block_rows[:, None] >= regions[None, :, 0]) & (
        block_rows[:, None] < regions[None, :, 1]
    )
    col_ok = (block_cols[:, None] >= regions[None, :, 2]) & (
        block_cols[:, None] < regions[None, :, 3]
    )
    valid = (row_ok[:, None, :] & col_ok[None, :, :]).reshape(1, tile_rows * tile_cols, agents)
    local_peak = jnp.max(jnp.where(valid, logits, -1e30), axis=1)
    peak = lax.pmax(local_peak, ("row", "col", "agent"))
    local_mass = jnp.sum(jnp.where(valid, jnp.exp(logits - peak[:, None, :]), 0.0), axis=1)
    mass = lax.psum(local_mass, ("row", "col", "agent"))
    normaliser = peak + jnp.log(mass)
    return (logits - normaliser[:, None, :]).reshape(scenes, tile_rows, tile_cols, agents)


def solution(mesh):
    in_specs = (
        P(None, "row", ("col", "agent"), None),
        P(),
        P(),
        P(),
        P(),
        P("agent", None),
        P(),
        P(),
    )
    out_specs = P(None, "row", ("col", "agent"), None)
    return jax.shard_map(shards, mesh=mesh, in_specs=in_specs, out_specs=out_specs, check_vma=False)
```

profile of v0, /device:TPU:0, one launch (start us, length us, event | category | flops | bytes accessed | tf_op | source)
XLA Modules:
  0.0 271.3 jit_solution(7832234871713748013)
XLA Ops:
  0.0 1.0 fusion.62
  1.0 1.3 collective-permute-start.1
  2.3 5.6 %collective-permute-start = (bf16[2,4,64,128]{3,2,1,0:T(8,128)(2,1)S(1)}, bf16[2,4,64,128]{3,2,1,0:T(8,128)(2,1)S(1)}, u32[]{:S(2)}, u32[]{:S(2)}) collective-permute-start(bf16[2,4,64,128]{3,2,1,0:T(8,128)(2,1)S(1)} %get-tuple-element.34), channel_id=1, source_target_pairs={{0,8},{8,16},{16,24},{1,9},{9,17},{17,25},{2,10},{10,18},{18,26},{... | collective-permute-start | bytes 393224 | tf_op jit(solution)/shard_map/ppermute | solution.py:14
  7.9 0.8 fusion.63
  8.8 0.1 compare_and_fusion
  8.9 0.1 compare_and_fusion.1
  9.0 1.7 collective-permute-done
  10.6 0.0 collective-permute-done.1
  10.6 9.2 %pad_maximum_fusion.4 = (bf16[2,128,64,128]{3,2,1,0:T(8,128)(2,1)}, bf16[2,136,64,128]{3,2,1,0:T(8,128)(2,1)S(1)}, bf16[2,128,64,128]{3,2,1,0:T(8,128)(2,1)S(1)}) fusion(bf16[2,4,64,128]{3,2,1,0:T(8,128)(2,1)S(1)} %collective-permute-done.1, bf16[2,128,64,128]{3,2,1,0:T(8,128)(2,1)} %param.8, ...), kind=kLoop, calls=%fused_computation.43 | loop fusion | flops 16777216 | bytes 17039360 | tf_op jit(solution)/shard_map/concatenate | solution.py:18
  19.9 0.2 fusion.60
  20.2 1.3 collective-permute-start.2
  21.5 1.3 collective-permute-start.3
  22.8 2.6 broadcast_and_fusion
  25.5 0.0 collective-permute-done.2
  25.5 0.1 copy.15
  25.6 1.3 collective-permute-done.3
  26.9 0.1 copy.17
  27.0 0.0 copy-start.11
  27.0 14.7 %pad_maximum_fusion.5 = (bf16[2,128,64,128]{3,2,1,0:T(8,128)(2,1)}, bf16[2,128,64,128]{3,2,1,0:T(8,128)(2,1)}, bf16[2,128,64,128]{3,2,1,0:T(8,128)(2,1)}, bf16[2...) fusion(bf16[2,136,64,128]{3,2,1,0:T(8,128)(2,1)S(1)} %constant_dynamic-u, ...), kind=kLoop, calls=%fused_computation.44 | loop fusion | flops 50331648 | bytes 30179328 | tf_op jit(solution)/shard_map/concatenate | solution.py:18
  41.7 1.2 fusion.27
  43.0 0.9 copy-done.10
  43.9 1.2 fusion.36
  45.1 1.2 convolution_add_fusion.13
  46.4 3.4 %convolution_add_fusion.12 = f32[16384,128]{1,0:T(8,128)S(1)} fusion(f32[16384,128]{1,0:T(8,128)S(1)} %convolution_add_fusion.13, bf16[16384,128]{1,0:T(8,128)(2,1)} %bitcast.119, bf16[3,3,128,128]{3,2,1,0:T(8,128)(2,1)S(1)} %copy-done.11), kind=kOutput, calls=%fused_computation.17 | convolution fusion | flops 538968064 | bytes 21004288 | tf_op jit(solution)/shard_map/dot_general | solution.py:34
  49.8 0.0 copy-start.5
  49.8 3.6 %convolution_add_fusion.11 = f32[16384,128]{1,0:T(8,128)S(1)} fusion(f32[16384,128]{1,0:T(8,128)S(1)} %convolution_add_fusion.12, bf16[16384,128]{1,0:T(8,128)(2,1)} %bitcast.118, bf16[3,3,128,128]{3,2,1,0:T(8,128)(2,1)S(1)} %copy-done.11), kind=kOutput, calls=%fused_computation.16 | convolution fusion | flops 538968064 | bytes 21004288 | tf_op jit(solution)/shard_map/dot_general | solution.py:34
  53.4 1.2 convolution_add_fusion.10
  54.7 1.2 convolution_add_fusion.9
  55.9 0.0 copy-start.15
  55.9 3.4 %convolution_add_fusion.8 = f32[16384,128]{1,0:T(8,128)S(1)} fusion(f32[16384,128]{1,0:T(8,128)S(1)} %convolution_add_fusion.9, bf16[16384,128]{1,0:T(8,128)(2,1)} %bitcast.116, bf16[3,3,128,128]{3,2,1,0:T(8,128)(2,1)S(1)} %copy-done.11), kind=kOutput, calls=%fused_computation.13 | convolution fusion | flops 538968064 | bytes 21004288 | tf_op jit(solution)/shard_map/dot_general | solution.py:34
  59.4 0.0 copy-start.13
  59.4 4.1 %fusion.7 = bf16[16384,128]{1,0:T(8,128)(2,1)S(1)} fusion(f32[16384,128]{1,0:T(8,128)S(1)} %fusion.27, f32[16384,128]{1,0:T(8,128)S(1)} %convolution_add_fusion.8, bf16[16384,128]{1,0:T(8,128)(2,1)} %bitcast.125, f32[128]{0:T(128)S(1)} %copy-done.15, bf16[3,3,128,128]{3,2,1,0:T(8,128)(2,1)S(1)} %copy-done.11), kind=kOutput, calls=%fused_computation.22 | convolution fusion | flops 547356672 | bytes 25199104 | tf_op jit(solution)/shard_map/dot_general | solution.py:34
  63.5 2.0 copy-done
  65.5 1.3 collective-permute-start.5
  66.8 5.0 %collective-permute-start.4 = (bf16[2,8,64,128]{3,2,1,0:T(8,128)(2,1)S(1)}, bf16[2,8,64,128]{3,2,1,0:T(8,128)(2,1)S(1)}, u32[]{:S(2)}, u32[]{:S(2)}) collective-permute-start(bf16[2,8,64,128]{3,2,1,0:T(8,128)(2,1)S(1)} %get-tuple-element.28), channel_id=1, source_target_pairs={{0,8},{8,16},{16,24},{1,9},{9,17},{17,25},{2,10},{10,18},{18,26},{... | collective-permute-start | bytes 786440 | tf_op jit(solution)/shard_map/ppermute | solution.py:14
  71.8 6.3 %all_gather.3 = bf16[256,128]{1,0:T(8,128)(2,1)S(1)} all-gather(bf16[128,128]{1,0:T(8,128)(2,1)S(1)} %copy-done.13), channel_id=1, replica_groups=mesh['row'=4,'col'=4,'agent'=2] {'agent'}, dimensions={0}, use_global_device_ids=true | all-gather | bytes 98304 | tf_op jit(solution)/shard_map/all_gather | solution.py:53
  78.2 0.9 gather_fusion
  79.1 1.5 pad_maximum_fusion.9
  80.6 2.9 %collective-permute-start.6 = (bf16[2,144,8,128]{3,2,1,0:T(8,128)(2,1)S(1)}, bf16[2,144,8,128]{3,2,1,0:T(8,128)(2,1)S(1)}, u32[]{:S(2)}, u32[]{:S(2)}) collective-permute-start(bf16[2,144,8,128]{3,2,1,0:T(8,128)(2,1)S(1)} %get-tuple-element.19), channel_id=1, source_target_pairs={{0,1},{1,2},{2,3},{3,4},{4,5},{5,6},{6,7},{8,9},{9,10},{10,11},{11... | collective-permute-start | bytes 1769480 | tf_op jit(solution)/shard_map/ppermute | solution.py:14
  83.5 0.0 copy-start.12
  83.5 1.4 collective-permute-start.7
  84.9 14.5 %pad_maximum_fusion.1 = (bf16[2,128,64,128]{3,2,1,0:T(8,128)(2,1)}, bf16[2,128,64,128]{3,2,1,0:T(8,128)(2,1)S(1)}) fusion(bf16[2,8,64,128]{3,2,1,0:T(8,128)(2,1)S(1)} %collective-permute-done.5, bf16[2,128,64,128]{3,2,1,0:T(8,128)(2,1)S(1)} %bitcast.105, bf16[2,8,64,128]{3,2,1,0:T(8,128)(2,1)S(1)} %collective-permute-done.4), kind=kLoop, calls=%fused_computation.40 | loop fusion | flops 4194304 | bytes 13107200 | tf_op jit(solution)/shard_map/concatenate | solution.py:18
  99.5 4.6 %fusion.24 = f32[16384,128]{1,0:T(8,128)} fusion(bf16[16384,128]{1,0:T(8,128)(2,1)S(1)} %bitcast.121, bf16[3,3,128,128]{3,2,1,0:T(8,128)(2,1)S(1)} %copy-done.12), kind=kOutput, calls=%fused_computation.64 | convolution fusion | flops 536870912 | bytes 12615680 | tf_op jit(solution)/shard_map/dot_general | solution.py:34
  104.1 7.8 %maximum_maximum_fusion = (bf16[2,144,72,128]{3,2,1,0:T(8,128)(2,1)}, bf16[2,144,72,128]{3,2,1,0:T(8,128)(2,1)}) fusion(bf16[2,8,64,128]{3,2,1,0:T(8,128)(2,1)S(1)} %collective-permute-done.5, bf16[2,128,64,128]{3,2,1,0:T(8,128)(2,1)S(1)} %bitcast.106, bf16[2,8,64,128]{3,2,1,0:T(8,128)(2,1)S(1)} %collective-permute-done.4, ...), kind=kLoop, calls=%fused_computation.30 | loop fusion | flops 42467328 | bytes 16515072 | tf_op jit(solution)/shard_map/concatenate | solution.py:18
  111.9 18.5 %fusion.58 = (bf16[2,128,64,128]{3,2,1,0:T(8,128)(2,1)}, bf16[2,128,64,128]{3,2,1,0:T(8,128)(2,1)}, bf16[2,128,64,128]{3,2,1,0:T(8,128)(2,1)}, bf16[2,128,64,128...) fusion(bf16[2,144,72,128]{3,2,1,0:T(8,128)(2,1)} %get-tuple-element.17, ...), kind=kLoop, calls=%fused_computation.113 | loop fusion | bytes 50331648 | tf_op jit(solution)/shard_map/slice | solution.py:28
  130.4 3.6 %fusion.16 = f32[16384,128]{1,0:T(8,128)S(1)} fusion(bf16[16384,128]{1,0:T(8,128)(2,1)} %bitcast.120, bf16[3,3,128,128]{3,2,1,0:T(8,128)(2,1)S(1)} %copy-done.12), kind=kOutput, calls=%fused_computation.56 | convolution fusion | flops 536870912 | bytes 12615680 | tf_op jit(solution)/shard_map/dot_general | solution.py:34
  134.0 1.1 copy-done.3
  135.0 1.2 copy-done.9
  136.2 1.2 convolution_add_fusion.6
  137.5 0.9 copy-done.8
  138.4 1.2 convolution_add_fusion.5
  139.7 0.9 copy-done.7
  140.6 1.2 convolution_add_fusion.4
  141.8 0.9 copy-done.2
  142.8 1.2 convolution_add_fusion.3
  144.0 3.6 %convolution_add_fusion.2 = f32[16384,128]{1,0:T(8,128)S(1)} fusion(f32[16384,128]{1,0:T(8,128)S(1)} %convolution_add_fusion.3, bf16[16384,128]{1,0:T(8,128)(2,1)} %bitcast.111, bf16[3,3,128,128]{3,2,1,0:T(8,128)(2,1)S(1)} %copy-done.12), kind=kOutput, calls=%fused_computation.5 | convolution fusion | flops 538968064 | bytes 21004288 | tf_op jit(solution)/shard_map/dot_general | solution.py:34
  147.6 0.0 copy-start.16
  147.6 1.2 convolution_add_fusion.1
  148.9 6.2 %fusion.6 = bf16[16384,128]{1,0:T(8,128)(2,1)} fusion(f32[16384,128]{1,0:T(8,128)S(1)} %fusion.16, f32[16384,128]{1,0:T(8,128)S(1)} %convolution_add_fusion.1, bf16[16384,128]{1,0:T(8,128)(2,1)} %bitcast.124, f32[128]{0:T(128)S(1)} %copy-done.16, bf16[3,3,128,128]{3,2,1,0:T(8,128)(2,1)S(1)} %copy-done.12), kind=kOutput, calls=%fused_computation.21 | convolution fusion | flops 547356672 | bytes 25199104 | tf_op jit(solution)/shard_map/dot_general | solution.py:34
  155.1 9.7 %select_reduce_fusion.1 = (f32[2,256]{1,0:T(2,128)S(1)}, f32[2,8192,256]{2,1,0:T(8,128)}) fusion(pred[8192,256]{1,0:T(8,128)(4,1)S(1)} %bitcast.107, bf16[2,8192,128]{2,1,0:T(8,128)(2,1)} %bitcast.126, bf16[256,128]{1,0:T(8,128)(2,1)S(1)} %gather_fusion, pred[256]{0:T(512)(128)(4,1)S(1)} %compare_and_fusion.2), kind=kOutput, calls=%fused_computation.24 | convolution fusion | flops 1082162688 | bytes 23136512 | tf_op jit(solution)/shard_map/snc,ac->sna/dot_general | solution.py:57
  164.8 45.7 %pmax.7 = f32[2,256]{1,0:T(2,128)S(1)} all-reduce(f32[2,256]{1,0:T(2,128)S(1)} %get-tuple-element.39), channel_id=1, replica_groups=mesh['row'=4,'col'=4,'agent'=2] {'row','col','agent'}, use_global_device_ids=true, to_apply=%region_1.2 | all-reduce | flops 512 | bytes 4096 | tf_op jit(solution)/shard_map/pmax | solution.py:68
  210.5 7.6 %select_reduce_fusion = f32[2,256]{1,0:T(2,128)S(1)} fusion(f32[2,8192,256]{2,1,0:T(8,128)} %get-tuple-element.40, f32[2,256]{1,0:T(2,128)S(1)} %pmax.7, pred[8192,256]{1,0:T(8,128)(4,1)S(1)} %bitcast.108), kind=kLoop, calls=%fused_computation.23 | loop fusion | flops 12582400 | bytes 18878464 | tf_op jit(solution)/shard_map/reduce_sum | solution.py:69
  218.1 41.5 %psum.7 = f32[2,256]{1,0:T(2,128)S(1)} all-reduce(f32[2,256]{1,0:T(2,128)S(1)} %select_reduce_fusion), channel_id=1, replica_groups=mesh['row'=4,'col'=4,'agent'=2] {'row','col','agent'}, use_global_device_ids=true, to_apply=%region_3.4 | all-reduce | flops 512 | bytes 4096 | tf_op jit(solution)/shard_map/psum | solution.py:70
  259.6 11.4 %broadcast_subtract_fusion = f32[2,8192,256]{2,1,0:T(8,128)} fusion(f32[2,8192,256]{2,1,0:T(8,128)} %get-tuple-element.40, f32[2,256]{1,0:T(2,128)S(1)} %log_add_fusion), kind=kLoop, calls=%fused_computation.25 | loop fusion | flops 4194304 | bytes 33556480 | tf_op jit(solution)/shard_map/sub | solution.py:72
  (36 shorter events, 0.2 us)
Async XLA Ops:
  1.0 9.6 %collective-permute-start.1 = (bf16[2,4,64,128]{3,2,1,0:T(8,128)(2,1)S(1)}, bf16[2,4,64,128]{3,2,1,0:T(8,128)(2,1)S(1)}, u32[]{:S(2)}, u32[]{:S(2)}) collective-permute-start(bf16[2,4,64,128]{3,2,1,0:T(8,128)(2,1)S(1)} %get-tuple-element.33), channel_id=1, source_target_pairs={{8,0},{16,8},{24,16},{9,1},{17,9},{25,17},{10,2},{18,10},{26,18},{... | collective-permute-start | bytes 393224 | tf_op jit(solution)/shard_map/ppermute | solution.py:17
  2.3 8.3 %collective-permute-start = (bf16[2,4,64,128]{3,2,1,0:T(8,128)(2,1)S(1)}, bf16[2,4,64,128]{3,2,1,0:T(8,128)(2,1)S(1)}, u32[]{:S(2)}, u32[]{:S(2)}) collective-permute-start(bf16[2,4,64,128]{3,2,1,0:T(8,128)(2,1)S(1)} %get-tuple-element.34), channel_id=1, source_target_pairs={{0,8},{8,16},{16,24},{1,9},{9,17},{17,25},{2,10},{10,18},{18,26},{... | collective-permute-start | bytes 393224 | tf_op jit(solution)/shard_map/ppermute | solution.py:14
  19.9 5.6 %copy-start.14 = (s32[256]{0:T(256)S(1)}, s32[256]{0:T(256)}, u32[]{:S(2)}) copy-start(s32[256]{0:T(256)} %param.14) | copy-start | bytes 3076
  20.2 5.3 %collective-permute-start.2 = (bf16[2,136,4,128]{3,1,2,0:T(8,128)(2,1)S(1)}, bf16[2,136,4,128]{3,1,2,0:T(8,128)(2,1)S(1)}, u32[]{:S(2)}, u32[]{:S(2)}) collective-permute-start(bf16[2,136,4,128]{3,1,2,0:T(8,128)(2,1)S(1)} %copy.14), channel_id=1, source_target_pairs={{0,1},{1,2},{2,3},{3,4},{4,5},{5,6},{6,7},{8,9},{9,10},{10,11},{11... | collective-permute-start | bytes 835592 | tf_op jit(solution)/shard_map/ppermute | solution.py:14
  21.5 5.4 %collective-permute-start.3 = (bf16[2,136,4,128]{3,1,2,0:T(8,128)(2,1)S(1)}, bf16[2,136,4,128]{3,1,2,0:T(8,128)(2,1)S(1)}, u32[]{:S(2)}, u32[]{:S(2)}) collective-permute-start(bf16[2,136,4,128]{3,1,2,0:T(8,128)(2,1)S(1)} %copy.16), channel_id=1, source_target_pairs={{1,0},{2,1},{3,2},{4,3},{5,4},{6,5},{7,6},{9,8},{10,9},{11,10},{12... | collective-permute-start | bytes 835592 | tf_op jit(solution)/shard_map/ppermute | solution.py:17
  27.0 14.7 %copy-start.11 = (bf16[3,3,128,128]{3,2,1,0:T(8,128)(2,1)S(1)}, bf16[3,3,128,128]{3,2,1,0:T(8,128)(2,1)}, u32[]{:S(2)}) copy-start(bf16[3,3,128,128]{3,2,1,0:T(8,128)(2,1)} %param.9) | copy-start | bytes 884740
  41.7 2.2 copy-start.10
  49.8 3.6 %copy-start.5 = (bf16[2,128,64,128]{3,2,1,0:T(8,128)(2,1)S(1)}, bf16[2,128,64,128]{3,2,1,0:T(8,128)(2,1)}, u32[]{:S(2)}) copy-start(bf16[2,128,64,128]{3,2,1,0:T(8,128)(2,1)} %param.8) | copy-start | bytes 12582916
  55.9 3.4 %copy-start.15 = (f32[128]{0:T(128)S(1)}, f32[128]{0:T(128)}, u32[]{:S(2)}) copy-start(f32[128]{0:T(128)} %param.10) | copy-start | bytes 1540
  59.4 12.5 %copy-start.13 = (bf16[128,128]{1,0:T(8,128)(2,1)S(1)}, bf16[128,128]{1,0:T(8,128)(2,1)}, u32[]{:S(2)}) copy-start(bf16[128,128]{1,0:T(8,128)(2,1)} %param.13) | copy-start | bytes 98308
  63.5 2.0 copy-start
  65.5 13.5 %collective-permute-start.5 = (bf16[2,8,64,128]{3,2,1,0:T(8,128)(2,1)S(1)}, bf16[2,8,64,128]{3,2,1,0:T(8,128)(2,1)S(1)}, u32[]{:S(2)}, u32[]{:S(2)}) collective-permute-start(bf16[2,8,64,128]{3,2,1,0:T(8,128)(2,1)S(1)} %get-tuple-element.29), channel_id=1, source_target_pairs={{8,0},{16,8},{24,16},{9,1},{17,9},{25,17},{10,2},{18,10},{26,18},{... | collective-permute-start | bytes 786440 | tf_op jit(solution)/shard_map/ppermute | solution.py:17
  66.8 12.2 %collective-permute-start.4 = (bf16[2,8,64,128]{3,2,1,0:T(8,128)(2,1)S(1)}, bf16[2,8,64,128]{3,2,1,0:T(8,128)(2,1)S(1)}, u32[]{:S(2)}, u32[]{:S(2)}) collective-permute-start(bf16[2,8,64,128]{3,2,1,0:T(8,128)(2,1)S(1)} %get-tuple-element.28), channel_id=1, source_target_pairs={{0,8},{8,16},{16,24},{1,9},{9,17},{17,25},{2,10},{10,18},{18,26},{... | collective-permute-start | bytes 786440 | tf_op jit(solution)/shard_map/ppermute | solution.py:14
  79.0 5.9 %copy-start.1 = (bf16[16384,128]{1,0:T(8,128)(2,1)S(1)}, bf16[16384,128]{1,0:T(8,128)(2,1)}, u32[]{:S(2)}) copy-start(bf16[16384,128]{1,0:T(8,128)(2,1)} %copy-done) | copy-start | bytes 12582916
  80.6 23.5 %collective-permute-start.6 = (bf16[2,144,8,128]{3,2,1,0:T(8,128)(2,1)S(1)}, bf16[2,144,8,128]{3,2,1,0:T(8,128)(2,1)S(1)}, u32[]{:S(2)}, u32[]{:S(2)}) collective-permute-start(bf16[2,144,8,128]{3,2,1,0:T(8,128)(2,1)S(1)} %get-tuple-element.19), channel_id=1, source_target_pairs={{0,1},{1,2},{2,3},{3,4},{4,5},{5,6},{6,7},{8,9},{9,10},{10,11},{11... | collective-permute-start | bytes 1769480 | tf_op jit(solution)/shard_map/ppermute | solution.py:14
  83.5 16.0 %copy-start.12 = (bf16[3,3,128,128]{3,2,1,0:T(8,128)(2,1)S(1)}, bf16[3,3,128,128]{3,2,1,0:T(8,128)(2,1)}, u32[]{:S(2)}) copy-start(bf16[3,3,128,128]{3,2,1,0:T(8,128)(2,1)} %param.11) | copy-start | bytes 884740
  83.5 20.6 %collective-permute-start.7 = (bf16[2,144,8,128]{3,2,1,0:T(8,128)(2,1)S(1)}, bf16[2,144,8,128]{3,2,1,0:T(8,128)(2,1)S(1)}, u32[]{:S(2)}, u32[]{:S(2)}) collective-permute-start(bf16[2,144,8,128]{3,2,1,0:T(8,128)(2,1)S(1)} %get-tuple-element.20), channel_id=1, source_target_pairs={{1,0},{2,1},{3,2},{4,3},{5,4},{6,5},{7,6},{9,8},{10,9},{11,10},{12... | collective-permute-start | bytes 1769480 | tf_op jit(solution)/shard_map/ppermute | solution.py:17
  130.4 4.6 %copy-start.3 = (f32[16384,128]{1,0:T(8,128)S(1)}, f32[16384,128]{1,0:T(8,128)}, u32[]{:S(2)}) copy-start(f32[16384,128]{1,0:T(8,128)} %fusion.24) | copy-start | bytes 25165828
  130.4 5.8 %copy-start.9 = (bf16[2,128,64,128]{3,2,1,0:T(8,128)(2,1)S(1)}, bf16[2,128,64,128]{3,2,1,0:T(8,128)(2,1)}, u32[]{:S(2)}) copy-start(bf16[2,128,64,128]{3,2,1,0:T(8,128)(2,1)} %get-tuple-element.7) | copy-start | bytes 12582916
  136.2 2.2 copy-start.8
  138.4 2.2 copy-start.7
  140.6 2.2 copy-start.2
  144.0 3.6 %copy-start.6 = (bf16[2,128,64,128]{3,2,1,0:T(8,128)(2,1)S(1)}, bf16[2,128,64,128]{3,2,1,0:T(8,128)(2,1)}, u32[]{:S(2)}) copy-start(bf16[2,128,64,128]{3,2,1,0:T(8,128)(2,1)} %get-tuple-element.5) | copy-start | bytes 12582916
  147.6 1.3 copy-start.16
  148.9 6.2 %copy-start.4 = (pred[128,64,256]{2,1,0:T(8,128)(4,1)S(1)}, pred[128,64,256]{2,1,0:T(8,128)(4,1)}, u32[]{:S(2)}) copy-start(pred[128,64,256]{2,1,0:T(8,128)(4,1)} %broadcast_and_fusion) | copy-start | bytes 6291460
where the time goes:
time: 277 us; the launch traced here: 271 us
  blocking collectives  93.5 us (34%)
  other arithmetic  69.7 us (25%)
  matrix products  54.6 us (20%)
  local copies, waits for them, and re-layouts  29.8 us (11%)
  starting transfers between devices  20.1 us (7%)
  waiting for transfers between devices  2.99 us (1%)
    concatenate x4, other arithmetic, padded_2(): block = jnp.concatenate([low, block, high], axis=dim)  46.2 us
    pmax x1, blocking collectives, shards(): peak = lax.pmax(local_peak, ('row', 'col', 'agent'))  45.7 us
    dot_general x18, matrix products, dilated(): jnp.dot(tap_piece.reshape(-1, channels), kernel[row_tap, col_tap], prefer...  44.9 us
    psum x1, blocking collectives, shards(): mass = lax.psum(local_mass, ('row', 'col', 'agent'))  41.5 us
    slice x1, local copies, waits for them, and re-layouts, dilated(): padded[:, row_tap * dilation:row_tap * dilation + out_rows, col_tap * dil...  18.5 us
    ppermute x4, starting transfers between devices, padded_2(): lax.ppermute(lax.slice_in_dim(block, block.shape[dim] - width, None, axis...  14.8 us
    sub x1, other arithmetic, shards(): logits - normaliser[:, None, :]  11.4 us
    dot_general x1, matrix products, shards(): jnp.einsum('snc,ac->sna', flat, ordered, preferred_element_type=jnp.float32)  9.68 us
  transfers between devices with their start and end apart: 8, of which 2 were waited for; matrix products, arithmetic and copies ran while one was open for 9% of the time, Pallas kernels for 0%

commit v1 on v0

--- a/solution.py
+++ b/solution.py
@@ -67,7 +67,8 @@
     local_peak = jnp.max(jnp.where(valid, logits, -1e30), axis=1)
     peak = lax.pmax(local_peak, ("row", "col", "agent"))
     local_mass = jnp.sum(jnp.where(valid, jnp.exp(logits - peak[:, None, :]), 0.0), axis=1)
-    mass = lax.psum(local_mass, ("row", "col", "agent"))
+    parts = lax.all_gather(local_mass, ("row", "col", "agent"), axis=0, tiled=False)
+    mass = parts.sum(axis=0)
     normaliser = peak + jnp.log(mass)
     return (logits - normaliser[:, None, :]).reshape(scenes, tile_rows, tile_cols, agents)
 

time: 277 us -> 268 us (0.968)
  other arithmetic: 69.7 us -> 57.6 us
  blocking collectives: 93.5 us -> 96.8 us
    all_gather x0 -> x1, blocking collectives: none -> 41.6 us  [shards(): lax.all_gather(local_mass, ('row', 'col', 'agent'), axis=0, tiled=False)]
    psum x1 -> x0, blocking collectives: 41.5 us -> none  [shards(): mass = lax.psum(local_mass, ('row', 'col', 'agent'))]
    concatenate x4, other arithmetic: 46.2 us -> 34.1 us  [padded_2(): block = jnp.concatenate([low, block, high], axis=dim)]
    pmax x1, blocking collectives: 45.7 us -> 48.9 us  [shards(): peak = lax.pmax(local_peak, ('row', 'col', 'agent'))]
  transfers between devices with their start and end apart: 8 -> 8, of which waited for: 2 -> 2; matrix products, arithmetic and copies ran while one was open for 9% -> 5% of each run, Pallas kernels for 0% -> 0%
where the time goes in v1:
time: 268 us; the launch traced here: 263 us
  blocking collectives  96.8 us (36%)
  other arithmetic  57.6 us (21%)
  matrix products  54.6 us (20%)
  local copies, waits for them, and re-layouts  29.8 us (11%)
  starting transfers between devices  20.1 us (8%)
  waiting for transfers between devices  2.99 us (1%)
    pmax x1, blocking collectives, shards(): peak = lax.pmax(local_peak, ('row', 'col', 'agent'))  48.9 us
    dot_general x18, matrix products, dilated(): jnp.dot(tap_piece.reshape(-1, channels), kernel[row_tap, col_tap], prefer...  44.9 us
    all_gather x1, blocking collectives, shards(): lax.all_gather(local_mass, ('row', 'col', 'agent'), axis=0, tiled=False)  41.6 us
    concatenate x4, other arithmetic, padded_2(): block = jnp.concatenate([low, block, high], axis=dim)  34.1 us
    slice x1, local copies, waits for them, and re-layouts, dilated(): padded[:, row_tap * dilation:row_tap * dilation + out_rows, col_tap * dil...  18.5 us
    ppermute x4, starting transfers between devices, padded_2(): lax.ppermute(lax.slice_in_dim(block, block.shape[dim] - width, None, axis...  14.8 us
    sub x1, other arithmetic, shards(): logits - normaliser[:, None, :]  11.4 us
    dot_general x1, matrix products, shards(): jnp.einsum('snc,ac->sna', flat, ordered, preferred_element_type=jnp.float32)  9.69 us
  transfers between devices with their start and end apart: 8, of which 2 were waited for; matrix products, arithmetic and copies ran while one was open for 5% of the time, Pallas kernels for 0%

profile of v1, /device:TPU:0, one launch (start us, length us, event | category | flops | bytes accessed | tf_op | source)
XLA Modules:
  0.0 262.7 jit_solution(15597294999027113523)
XLA Ops:
  0.0 1.0 fusion.62
  1.0 1.3 collective-permute-start.1
  2.3 5.6 %collective-permute-start = (bf16[2,4,64,128]{3,2,1,0:T(8,128)(2,1)S(1)}, bf16[2,4,64,128]{3,2,1,0:T(8,128)(2,1)S(1)}, u32[]{:S(2)}, u32[]{:S(2)}) collective-permute-start(bf16[2,4,64,128]{3,2,1,0:T(8,128)(2,1)S(1)} %get-tuple-element.34), channel_id=1, source_target_pairs={{0,8},{8,16},{16,24},{1,9},{9,17},{17,25},{2,10},{10,18},{18,26},{... | collective-permute-start | bytes 393224 | tf_op jit(solution)/shard_map/ppermute | solution.py:14
  7.9 0.8 fusion.63
  8.8 0.1 compare_and_fusion
  8.9 0.1 compare_and_fusion.1
  9.0 1.7 collective-permute-done
  10.6 9.2 %pad_maximum_fusion.4 = (bf16[2,128,64,128]{3,2,1,0:T(8,128)(2,1)}, bf16[2,136,64,128]{3,2,1,0:T(8,128)(2,1)S(1)}, bf16[2,128,64,128]{3,2,1,0:T(8,128)(2,1)S(1)}) fusion(bf16[2,4,64,128]{3,2,1,0:T(8,128)(2,1)S(1)} %collective-permute-done.1, bf16[2,128,64,128]{3,2,1,0:T(8,128)(2,1)} %param.8, ...), kind=kLoop, calls=%fused_computation.43 | loop fusion | flops 16777216 | bytes 17039360 | tf_op jit(solution)/shard_map/concatenate | solution.py:18
  19.9 0.2 fusion.60
  20.2 1.3 collective-permute-start.2
  21.5 1.3 collective-permute-start.3
  22.8 2.6 %broadcast_and_fusion = pred[128,64,256]{2,1,0:T(8,128)(4,1)} fusion(pred[64,256]{1,0:T(8,128)(4,1)S(1)} %compare_and_fusion.1, pred[128,256]{1,0:T(8,128)(4,1)S(1)} %compare_and_fusion), kind=kLoop, calls=%fused_computation.46 | loop fusion | flops 2097152 | bytes 2146304 | tf_op jit(solution)/shard_map/and | solution.py:66
  25.5 0.1 copy.15
  25.6 1.3 collective-permute-done.3
  26.9 0.1 copy.17
  27.0 0.0 copy-start.11
  27.0 14.5 %pad_maximum_fusion.5 = (bf16[2,128,64,128]{3,2,1,0:T(8,128)(2,1)}, bf16[2,128,64,128]{3,2,1,0:T(8,128)(2,1)}, bf16[2,128,64,128]{3,2,1,0:T(8,128)(2,1)}, bf16[2...) fusion(bf16[2,136,64,128]{3,2,1,0:T(8,128)(2,1)S(1)} %constant_dynamic-u, ...), kind=kLoop, calls=%fused_computation.44 | loop fusion | flops 50331648 | bytes 30179328 | tf_op jit(solution)/shard_map/concatenate | solution.py:18
  41.5 1.2 fusion.27
  42.8 0.9 copy-done.10
  43.7 1.2 fusion.36
  44.9 1.2 convolution_add_fusion.13
  46.2 3.4 %convolution_add_fusion.12 = f32[16384,128]{1,0:T(8,128)S(1)} fusion(f32[16384,128]{1,0:T(8,128)S(1)} %convolution_add_fusion.13, bf16[16384,128]{1,0:T(8,128)(2,1)} %bitcast.120, bf16[3,3,128,128]{3,2,1,0:T(8,128)(2,1)S(1)} %copy-done.11), kind=kOutput, calls=%fused_computation.17 | convolution fusion | flops 538968064 | bytes 21004288 | tf_op jit(solution)/shard_map/dot_general | solution.py:34
  49.6 0.0 copy-start.5
  49.6 3.6 %convolution_add_fusion.11 = f32[16384,128]{1,0:T(8,128)S(1)} fusion(f32[16384,128]{1,0:T(8,128)S(1)} %convolution_add_fusion.12, bf16[16384,128]{1,0:T(8,128)(2,1)} %bitcast.119, bf16[3,3,128,128]{3,2,1,0:T(8,128)(2,1)S(1)} %copy-done.11), kind=kOutput, calls=%fused_computation.16 | convolution fusion | flops 538968064 | bytes 21004288 | tf_op jit(solution)/shard_map/dot_general | solution.py:34
  53.2 1.2 convolution_add_fusion.10
  54.5 1.2 convolution_add_fusion.9
  55.7 0.0 copy-start.15
  55.7 3.4 %convolution_add_fusion.8 = f32[16384,128]{1,0:T(8,128)S(1)} fusion(f32[16384,128]{1,0:T(8,128)S(1)} %convolution_add_fusion.9, bf16[16384,128]{1,0:T(8,128)(2,1)} %bitcast.117, bf16[3,3,128,128]{3,2,1,0:T(8,128)(2,1)S(1)} %copy-done.11), kind=kOutput, calls=%fused_computation.13 | convolution fusion | flops 538968064 | bytes 21004288 | tf_op jit(solution)/shard_map/dot_general | solution.py:34
  59.2 0.0 copy-start.13
  59.2 4.1 %fusion.7 = bf16[16384,128]{1,0:T(8,128)(2,1)S(1)} fusion(f32[16384,128]{1,0:T(8,128)S(1)} %fusion.27, f32[16384,128]{1,0:T(8,128)S(1)} %convolution_add_fusion.8, bf16[16384,128]{1,0:T(8,128)(2,1)} %bitcast.126, f32[128]{0:T(128)S(1)} %copy-done.15, bf16[3,3,128,128]{3,2,1,0:T(8,128)(2,1)S(1)} %copy-done.11), kind=kOutput, calls=%fused_computation.22 | convolution fusion | flops 547356672 | bytes 25199104 | tf_op jit(solution)/shard_map/dot_general | solution.py:34
  63.3 2.0 copy-done
  65.3 1.3 collective-permute-start.5
  66.6 5.0 %collective-permute-start.4 = (bf16[2,8,64,128]{3,2,1,0:T(8,128)(2,1)S(1)}, bf16[2,8,64,128]{3,2,1,0:T(8,128)(2,1)S(1)}, u32[]{:S(2)}, u32[]{:S(2)}) collective-permute-start(bf16[2,8,64,128]{3,2,1,0:T(8,128)(2,1)S(1)} %get-tuple-element.28), channel_id=1, source_target_pairs={{0,8},{8,16},{16,24},{1,9},{9,17},{17,25},{2,10},{10,18},{18,26},{... | collective-permute-start | bytes 786440 | tf_op jit(solution)/shard_map/ppermute | solution.py:14
  71.6 6.3 %all_gather.9 = bf16[256,128]{1,0:T(8,128)(2,1)S(1)} all-gather(bf16[128,128]{1,0:T(8,128)(2,1)S(1)} %copy-done.13), channel_id=1, replica_groups=mesh['row'=4,'col'=4,'agent'=2] {'agent'}, dimensions={0}, use_global_device_ids=true | all-gather | bytes 98304 | tf_op jit(solution)/shard_map/all_gather | solution.py:53
  78.0 0.9 gather_fusion
  78.8 0.0 collective-permute-done.5
  78.8 0.0 collective-permute-done.4
  78.9 1.5 pad_maximum_fusion.9
  80.4 2.9 %collective-permute-start.6 = (bf16[2,144,8,128]{3,2,1,0:T(8,128)(2,1)S(1)}, bf16[2,144,8,128]{3,2,1,0:T(8,128)(2,1)S(1)}, u32[]{:S(2)}, u32[]{:S(2)}) collective-permute-start(bf16[2,144,8,128]{3,2,1,0:T(8,128)(2,1)S(1)} %get-tuple-element.19), channel_id=1, source_target_pairs={{0,1},{1,2},{2,3},{3,4},{4,5},{5,6},{6,7},{8,9},{9,10},{10,11},{11... | collective-permute-start | bytes 1769480 | tf_op jit(solution)/shard_map/ppermute | solution.py:14
  83.3 0.0 copy-start.12
  83.3 1.4 collective-permute-start.7
  84.7 2.7 %pad_maximum_fusion.1 = (bf16[2,128,64,128]{3,2,1,0:T(8,128)(2,1)}, bf16[2,128,64,128]{3,2,1,0:T(8,128)(2,1)S(1)}) fusion(bf16[2,8,64,128]{3,2,1,0:T(8,128)(2,1)S(1)} %collective-permute-done.5, bf16[2,128,64,128]{3,2,1,0:T(8,128)(2,1)S(1)} %bitcast.106, bf16[2,8,64,128]{3,2,1,0:T(8,128)(2,1)S(1)} %collective-permute-done.4), kind=kLoop, calls=%fused_computation.40 | loop fusion | flops 4194304 | bytes 13107200 | tf_op jit(solution)/shard_map/concatenate | solution.py:18
  87.4 4.6 %fusion.24 = f32[16384,128]{1,0:T(8,128)} fusion(bf16[16384,128]{1,0:T(8,128)(2,1)S(1)} %bitcast.122, bf16[3,3,128,128]{3,2,1,0:T(8,128)(2,1)S(1)} %copy-done.12), kind=kOutput, calls=%fused_computation.64 | convolution fusion | flops 536870912 | bytes 12615680 | tf_op jit(solution)/shard_map/dot_general | solution.py:34
  92.0 7.8 %maximum_maximum_fusion = (bf16[2,144,72,128]{3,2,1,0:T(8,128)(2,1)}, bf16[2,144,72,128]{3,2,1,0:T(8,128)(2,1)}) fusion(bf16[2,8,64,128]{3,2,1,0:T(8,128)(2,1)S(1)} %collective-permute-done.5, bf16[2,128,64,128]{3,2,1,0:T(8,128)(2,1)S(1)} %bitcast.107, bf16[2,8,64,128]{3,2,1,0:T(8,128)(2,1)S(1)} %collective-permute-done.4, ...), kind=kLoop, calls=%fused_computation.30 | loop fusion | flops 42467328 | bytes 16515072 | tf_op jit(solution)/shard_map/concatenate | solution.py:18
  99.8 18.5 %fusion.58 = (bf16[2,128,64,128]{3,2,1,0:T(8,128)(2,1)}, bf16[2,128,64,128]{3,2,1,0:T(8,128)(2,1)}, bf16[2,128,64,128]{3,2,1,0:T(8,128)(2,1)}, bf16[2,128,64,128...) fusion(bf16[2,144,72,128]{3,2,1,0:T(8,128)(2,1)} %get-tuple-element.17, ...), kind=kLoop, calls=%fused_computation.113 | loop fusion | bytes 50331648 | tf_op jit(solution)/shard_map/slice | solution.py:28
  118.3 3.6 %fusion.16 = f32[16384,128]{1,0:T(8,128)S(1)} fusion(bf16[16384,128]{1,0:T(8,128)(2,1)} %bitcast.121, bf16[3,3,128,128]{3,2,1,0:T(8,128)(2,1)S(1)} %copy-done.12), kind=kOutput, calls=%fused_computation.56 | convolution fusion | flops 536870912 | bytes 12615680 | tf_op jit(solution)/shard_map/dot_general | solution.py:34
  121.9 1.1 copy-done.3
  123.0 1.2 copy-done.9
  124.2 1.2 convolution_add_fusion.6
  125.4 0.9 copy-done.8
  126.3 1.2 convolution_add_fusion.5
  127.6 0.9 copy-done.7
  128.5 1.2 convolution_add_fusion.4
  129.8 0.9 copy-done.2
  130.7 1.2 convolution_add_fusion.3
  132.0 3.6 %convolution_add_fusion.2 = f32[16384,128]{1,0:T(8,128)S(1)} fusion(f32[16384,128]{1,0:T(8,128)S(1)} %convolution_add_fusion.3, bf16[16384,128]{1,0:T(8,128)(2,1)} %bitcast.112, bf16[3,3,128,128]{3,2,1,0:T(8,128)(2,1)S(1)} %copy-done.12), kind=kOutput, calls=%fused_computation.5 | convolution fusion | flops 538968064 | bytes 21004288 | tf_op jit(solution)/shard_map/dot_general | solution.py:34
  135.6 0.0 copy-start.16
  135.6 1.2 convolution_add_fusion.1
  136.8 6.2 %fusion.6 = bf16[16384,128]{1,0:T(8,128)(2,1)} fusion(f32[16384,128]{1,0:T(8,128)S(1)} %fusion.16, f32[16384,128]{1,0:T(8,128)S(1)} %convolution_add_fusion.1, bf16[16384,128]{1,0:T(8,128)(2,1)} %bitcast.125, f32[128]{0:T(128)S(1)} %copy-done.16, bf16[3,3,128,128]{3,2,1,0:T(8,128)(2,1)S(1)} %copy-done.12), kind=kOutput, calls=%fused_computation.21 | convolution fusion | flops 547356672 | bytes 25199104 | tf_op jit(solution)/shard_map/dot_general | solution.py:34
  143.1 9.7 %select_reduce_fusion.1 = (f32[2,256]{1,0:T(2,128)S(1)}, f32[2,8192,256]{2,1,0:T(8,128)}) fusion(pred[8192,256]{1,0:T(8,128)(4,1)S(1)} %bitcast.108, bf16[2,8192,128]{2,1,0:T(8,128)(2,1)} %bitcast.127, bf16[256,128]{1,0:T(8,128)(2,1)S(1)} %gather_fusion, pred[256]{0:T(512)(128)(4,1)S(1)} %compare_and_fusion.2), kind=kOutput, calls=%fused_computation.24 | convolution fusion | flops 1082162688 | bytes 23136512 | tf_op jit(solution)/shard_map/snc,ac->sna/dot_general | solution.py:57
  152.7 48.9 %pmax.7 = f32[2,256]{1,0:T(2,128)S(1)} all-reduce(f32[2,256]{1,0:T(2,128)S(1)} %get-tuple-element.39), channel_id=1, replica_groups=mesh['row'=4,'col'=4,'agent'=2] {'row','col','agent'}, use_global_device_ids=true, to_apply=%region_1.2 | all-reduce | flops 512 | bytes 4096 | tf_op jit(solution)/shard_map/pmax | solution.py:68
  201.6 7.6 %select_reduce_fusion = f32[2,256]{1,0:T(2,128)S(1)} fusion(f32[2,8192,256]{2,1,0:T(8,128)} %get-tuple-element.40, f32[2,256]{1,0:T(2,128)S(1)} %pmax.7, pred[8192,256]{1,0:T(8,128)(4,1)S(1)} %bitcast.109), kind=kLoop, calls=%fused_computation.23 | loop fusion | flops 12582400 | bytes 18878464 | tf_op jit(solution)/shard_map/reduce_sum | solution.py:69
  209.3 41.6 %all-gather.1 = f32[32,2,256]{2,1,0:T(2,128)S(1)} all-gather(f32[1,2,256]{2,1,0:T(2,128)S(1)} %bitcast.128), channel_id=2, replica_groups=mesh['row'=4,'col'=4,'agent'=2] {'row','col','agent'}, dimensions={0}, use_global_device_ids=true | all-gather | bytes 67584 | tf_op jit(solution)/shard_map/all_gather | solution.py:70
  250.9 11.4 %broadcast_subtract_fusion = f32[2,8192,256]{2,1,0:T(8,128)} fusion(f32[2,8192,256]{2,1,0:T(8,128)} %get-tuple-element.40, f32[2,256]{1,0:T(2,128)S(1)} %log_add_fusion), kind=kLoop, calls=%fused_computation.25 | loop fusion | flops 4194304 | bytes 33556480 | tf_op jit(solution)/shard_map/sub | solution.py:73
  (37 shorter events, 0.3 us)
Async XLA Ops:
  1.0 9.6 %collective-permute-start.1 = (bf16[2,4,64,128]{3,2,1,0:T(8,128)(2,1)S(1)}, bf16[2,4,64,128]{3,2,1,0:T(8,128)(2,1)S(1)}, u32[]{:S(2)}, u32[]{:S(2)}) collective-permute-start(bf16[2,4,64,128]{3,2,1,0:T(8,128)(2,1)S(1)} %get-tuple-element.33), channel_id=1, source_target_pairs={{8,0},{16,8},{24,16},{9,1},{17,9},{25,17},{10,2},{18,10},{26,18},{... | collective-permute-start | bytes 393224 | tf_op jit(solution)/shard_map/ppermute | solution.py:17
  2.3 8.3 %collective-permute-start = (bf16[2,4,64,128]{3,2,1,0:T(8,128)(2,1)S(1)}, bf16[2,4,64,128]{3,2,1,0:T(8,128)(2,1)S(1)}, u32[]{:S(2)}, u32[]{:S(2)}) collective-permute-start(bf16[2,4,64,128]{3,2,1,0:T(8,128)(2,1)S(1)} %get-tuple-element.34), channel_id=1, source_target_pairs={{0,8},{8,16},{16,24},{1,9},{9,17},{17,25},{2,10},{10,18},{18,26},{... | collective-permute-start | bytes 393224 | tf_op jit(solution)/shard_map/ppermute | solution.py:14
  19.9 5.6 %copy-start.14 = (s32[256]{0:T(256)S(1)}, s32[256]{0:T(256)}, u32[]{:S(2)}) copy-start(s32[256]{0:T(256)} %param.14) | copy-start | bytes 3076
  20.2 5.3 %collective-permute-start.2 = (bf16[2,136,4,128]{3,1,2,0:T(8,128)(2,1)S(1)}, bf16[2,136,4,128]{3,1,2,0:T(8,128)(2,1)S(1)}, u32[]{:S(2)}, u32[]{:S(2)}) collective-permute-start(bf16[2,136,4,128]{3,1,2,0:T(8,128)(2,1)S(1)} %copy.14), channel_id=1, source_target_pairs={{0,1},{1,2},{2,3},{3,4},{4,5},{5,6},{6,7},{8,9},{9,10},{10,11},{11... | collective-permute-start | bytes 835592 | tf_op jit(solution)/shard_map/ppermute | solution.py:14
  21.5 5.4 %collective-permute-start.3 = (bf16[2,136,4,128]{3,1,2,0:T(8,128)(2,1)S(1)}, bf16[2,136,4,128]{3,1,2,0:T(8,128)(2,1)S(1)}, u32[]{:S(2)}, u32[]{:S(2)}) collective-permute-start(bf16[2,136,4,128]{3,1,2,0:T(8,128)(2,1)S(1)} %copy.16), channel_id=1, source_target_pairs={{1,0},{2,1},{3,2},{4,3},{5,4},{6,5},{7,6},{9,8},{10,9},{11,10},{12... | collective-permute-start | bytes 835592 | tf_op jit(solution)/shard_map/ppermute | solution.py:17
  27.0 14.5 %copy-start.11 = (bf16[3,3,128,128]{3,2,1,0:T(8,128)(2,1)S(1)}, bf16[3,3,128,128]{3,2,1,0:T(8,128)(2,1)}, u32[]{:S(2)}) copy-start(bf16[3,3,128,128]{3,2,1,0:T(8,128)(2,1)} %param.9) | copy-start | bytes 884740
  41.5 2.2 copy-start.10
  49.6 3.6 %copy-start.5 = (bf16[2,128,64,128]{3,2,1,0:T(8,128)(2,1)S(1)}, bf16[2,128,64,128]{3,2,1,0:T(8,128)(2,1)}, u32[]{:S(2)}) copy-start(bf16[2,128,64,128]{3,2,1,0:T(8,128)(2,1)} %param.8) | copy-start | bytes 12582916
  55.7 3.4 %copy-start.15 = (f32[128]{0:T(128)S(1)}, f32[128]{0:T(128)}, u32[]{:S(2)}) copy-start(f32[128]{0:T(128)} %param.10) | copy-start | bytes 1540
  59.2 12.5 %copy-start.13 = (bf16[128,128]{1,0:T(8,128)(2,1)S(1)}, bf16[128,128]{1,0:T(8,128)(2,1)}, u32[]{:S(2)}) copy-start(bf16[128,128]{1,0:T(8,128)(2,1)} %param.13) | copy-start | bytes 98308
  63.3 2.0 copy-start
  65.3 13.5 %collective-permute-start.5 = (bf16[2,8,64,128]{3,2,1,0:T(8,128)(2,1)S(1)}, bf16[2,8,64,128]{3,2,1,0:T(8,128)(2,1)S(1)}, u32[]{:S(2)}, u32[]{:S(2)}) collective-permute-start(bf16[2,8,64,128]{3,2,1,0:T(8,128)(2,1)S(1)} %get-tuple-element.29), channel_id=1, source_target_pairs={{8,0},{16,8},{24,16},{9,1},{17,9},{25,17},{10,2},{18,10},{26,18},{... | collective-permute-start | bytes 786440 | tf_op jit(solution)/shard_map/ppermute | solution.py:17
  66.6 12.2 %collective-permute-start.4 = (bf16[2,8,64,128]{3,2,1,0:T(8,128)(2,1)S(1)}, bf16[2,8,64,128]{3,2,1,0:T(8,128)(2,1)S(1)}, u32[]{:S(2)}, u32[]{:S(2)}) collective-permute-start(bf16[2,8,64,128]{3,2,1,0:T(8,128)(2,1)S(1)} %get-tuple-element.28), channel_id=1, source_target_pairs={{0,8},{8,16},{16,24},{1,9},{9,17},{17,25},{2,10},{10,18},{18,26},{... | collective-permute-start | bytes 786440 | tf_op jit(solution)/shard_map/ppermute | solution.py:14
  78.8 5.9 %copy-start.1 = (bf16[16384,128]{1,0:T(8,128)(2,1)S(1)}, bf16[16384,128]{1,0:T(8,128)(2,1)}, u32[]{:S(2)}) copy-start(bf16[16384,128]{1,0:T(8,128)(2,1)} %copy-done) | copy-start | bytes 12582916
  80.4 11.7 %collective-permute-start.6 = (bf16[2,144,8,128]{3,2,1,0:T(8,128)(2,1)S(1)}, bf16[2,144,8,128]{3,2,1,0:T(8,128)(2,1)S(1)}, u32[]{:S(2)}, u32[]{:S(2)}) collective-permute-start(bf16[2,144,8,128]{3,2,1,0:T(8,128)(2,1)S(1)} %get-tuple-element.19), channel_id=1, source_target_pairs={{0,1},{1,2},{2,3},{3,4},{4,5},{5,6},{6,7},{8,9},{9,10},{10,11},{11... | collective-permute-start | bytes 1769480 | tf_op jit(solution)/shard_map/ppermute | solution.py:14
  83.3 4.1 %copy-start.12 = (bf16[3,3,128,128]{3,2,1,0:T(8,128)(2,1)S(1)}, bf16[3,3,128,128]{3,2,1,0:T(8,128)(2,1)}, u32[]{:S(2)}) copy-start(bf16[3,3,128,128]{3,2,1,0:T(8,128)(2,1)} %param.11) | copy-start | bytes 884740
  83.3 8.7 %collective-permute-start.7 = (bf16[2,144,8,128]{3,2,1,0:T(8,128)(2,1)S(1)}, bf16[2,144,8,128]{3,2,1,0:T(8,128)(2,1)S(1)}, u32[]{:S(2)}, u32[]{:S(2)}) collective-permute-start(bf16[2,144,8,128]{3,2,1,0:T(8,128)(2,1)S(1)} %get-tuple-element.20), channel_id=1, source_target_pairs={{1,0},{2,1},{3,2},{4,3},{5,4},{6,5},{7,6},{9,8},{10,9},{11,10},{12... | collective-permute-start | bytes 1769480 | tf_op jit(solution)/shard_map/ppermute | solution.py:17
  118.3 4.6 %copy-start.3 = (f32[16384,128]{1,0:T(8,128)S(1)}, f32[16384,128]{1,0:T(8,128)}, u32[]{:S(2)}) copy-start(f32[16384,128]{1,0:T(8,128)} %fusion.24) | copy-start | bytes 25165828
  118.3 5.8 %copy-start.9 = (bf16[2,128,64,128]{3,2,1,0:T(8,128)(2,1)S(1)}, bf16[2,128,64,128]{3,2,1,0:T(8,128)(2,1)}, u32[]{:S(2)}) copy-start(bf16[2,128,64,128]{3,2,1,0:T(8,128)(2,1)} %get-tuple-element.7) | copy-start | bytes 12582916
  124.1 2.2 copy-start.8
  126.3 2.2 copy-start.7
  128.5 2.2 copy-start.2
  132.0 3.6 %copy-start.6 = (bf16[2,128,64,128]{3,2,1,0:T(8,128)(2,1)S(1)}, bf16[2,128,64,128]{3,2,1,0:T(8,128)(2,1)}, u32[]{:S(2)}) copy-start(bf16[2,128,64,128]{3,2,1,0:T(8,128)(2,1)} %get-tuple-element.5) | copy-start | bytes 12582916
  135.6 1.3 copy-start.16
  136.8 6.2 %copy-start.4 = (pred[128,64,256]{2,1,0:T(8,128)(4,1)S(1)}, pred[128,64,256]{2,1,0:T(8,128)(4,1)}, u32[]{:S(2)}) copy-start(pred[128,64,256]{2,1,0:T(8,128)(4,1)} %broadcast_and_fusion) | copy-start | bytes 6291460
